TPU v7x, 256 devices: a whole 4x4x8 slice. The times are simulated.
256 devices in a mesh: particle: 16 (over y, z_hi), coeffici: 8 (over x, core), half: 2 (over z_lo).
Axes of the slice: x: 4, y: 4, z: 8 (z_hi: 4, z_lo: 2; z = z_hi * 2 + z_lo), core: 2. Of those that a mesh axis runs over, the one named last changes fastest.
Arguments:
- residuals: float32 [2, 16384, 16384], P('half', 'particle', 'coeffici'), may hold values from -6 to 6
- loadings: float32 [2, 16384, 256], P('half', 'coeffici'), may hold values from -0.046875 to 0.046875
Outputs:
- new_loadings: float32 [2, 16384, 256], P('half', ('coeffici', 'particle'))
- rayleigh: float32 [2, 256, 256], P('half')
All inputs are finite; a program needn't handle non-finite values.
Results may differ from a plain program's by a relative error of at most 0.00024.
Values sent between devices are 32-bit elements; how exact they have to be, the bound alone decides.
No kernel may reach another device: no remote copies, remote signals or barrier semaphores. Data moves between devices by JAX's collectives and lax.ppermute only.
A program may use at most 64 MiB of HBM per device.

v0:
```python
import math
import jax
import jax.numpy as jnp
from jax import lax
from jax.sharding import PartitionSpec as P


def from_partner(value, axis, distance):
    mask = 2**distance
    pairs = [(source, source ^ mask) for source in range(lax.axis_size(axis))]
    return lax.ppermute(value, axis, pairs)


def contract_rows(left, right):
    return lax.dot_general(
        left,
        right,
        (((0,), (0,)), ((), ())),
        precision=lax.Precision.HIGHEST,
        preferred_element_type=jnp.float32,
    )


def local(residuals, loadings):
    samples = residuals[0]
    loading = loadings[0]
    factor = 1.0 / math.sqrt(samples.shape[0] * lax.axis_size("particle"))
    partial_value = jnp.dot(
        samples, loading, precision=lax.Precision.HIGHEST, preferred_element_type=jnp.float32
    )
    scores = lax.psum(partial_value, "coeffici")
    share_rows = samples.shape[1] // lax.axis_size("particle")
    first_row = lax.axis_index("particle") * share_rows
    local_cov = contract_rows(samples, scores)
    covariance = lax.psum(local_cov, "particle") * factor
    partner = from_partner(covariance, "half", 0)
    shrunk = covariance * jax.nn.sigmoid(covariance * partner)
    correlation = contract_rows(loading, shrunk)
    rayleigh = lax.psum(correlation, "coeffici") * factor
    weighted = lax.dynamic_slice_in_dim(shrunk, first_row, share_rows, 0)
    return (weighted[None], rayleigh[None])


def solution(mesh):
    in_specs = (P("half", "particle", "coeffici"), P("half", "coeffici", None))
    out_specs = (P("half", ("coeffici", "particle"), None), P("half", None, None))
    return jax.shard_map(local, mesh=mesh, in_specs=in_specs, out_specs=out_specs, check_vma=False)
```

profile of v0, /device:TPU:8, one launch (start us, length us, event | category | flops | bytes accessed | tf_op | source)
XLA Modules:
  0.0 395.9 jit_solution(12921856936748713425)
XLA Ops:
  7.2 0.0 copy-start
  7.2 0.0 all-reduce.4.cloned.1.call-start
  7.2 1.5 copy-done
  8.8 9.9 %fusion.2 = f32[1024,256]{1,0:T(8,128)} fusion(f32[1,1024,2048]{2,1,0:T(8,128)} %param.2, f32[1,2048,256]{2,1,0:T(8,128)S(1)} %copy-done), kind=kOutput, calls=%fused_computation.2 | convolution fusion | flops 6442450944 | bytes 11534336 | tf_op jit(solution)/shard_map/dot_general | solution.py:28
  18.6 0.0 all-reduce.4.cloned.1.call-update
  18.7 0.0 all-reduce.6.cloned.1.call-start
  18.7 70.6 %all-reduce.4.cloned.1.call-done = f32[1024,256]{1,0:T(8,128)} async-done(((f32[1024,256]{1,0:T(8,128)}), f32[1024,256]{1,0:T(8,128)}) %all-reduce.4.cloned.1.call-update) | async-done | bytes 1048592 | tf_op jit(solution)/shard_map/psum | solution.py:31
  89.3 10.7 %fusion.4 = f32[2048,256]{0,1:T(8,128)} fusion(f32[1024,256]{1,0:T(8,128)} %all-reduce.4.cloned.1.call-done, f32[1,1024,2048]{2,1,0:T(8,128)} %param.2), kind=kOutput, calls=%fused_computation.4 | convolution fusion | flops 6442450944 | bytes 11534336 | tf_op jit(solution)/shard_map/dot_general | solution.py:15
  100.1 0.0 all-reduce.6.cloned.1.call-update
  100.1 0.0 all-reduce.8.cloned.1.call-start
  100.1 175.1 %all-reduce.6.cloned.1.call-done = f32[2048,256]{0,1:T(8,128)} async-done(((f32[2048,256]{0,1:T(8,128)}), f32[2048,256]{0,1:T(8,128)}) %all-reduce.6.cloned.1.call-update) | async-done | bytes 2097168 | tf_op jit(solution)/shard_map/psum | solution.py:35
  275.3 1.9 broadcast_multiply_fusion
  277.2 2.2 collective-permute-start
  279.3 38.0 %collective-permute-done = f32[2048,256]{0,1:T(8,128)S(1)} collective-permute-done((f32[2048,256]{0,1:T(8,128)S(1)}, f32[2048,256]{0,1:T(8,128)S(1)}, u32[]{:S(2)}, u32[]{:S(2)}) %collective-permute-start) | collective-permute-done | bytes 2097184 | tf_op jit(solution)/shard_map/ppermute | solution.py:11
  317.3 0.0 copy-done.2
  317.3 0.9 divide_multiply_fusion
  318.3 1.3 copy-done.1
  319.6 2.6 fusion.10
  322.2 0.0 all-reduce.8.cloned.1.call-update
  322.2 0.9 constant_dynamic-slice_fusion
  323.2 0.8 copy.5
  323.9 63.6 %all-reduce.8.cloned.1.call-done = f32[256,256]{0,1:T(8,128)} async-done(((f32[256,256]{0,1:T(8,128)}), f32[256,256]{0,1:T(8,128)}) %all-reduce.8.cloned.1.call-update) | async-done | bytes 262160 | tf_op jit(solution)/shard_map/psum | solution.py:39
  387.5 1.0 multiply_bitcast_fusion
  388.5 0.8 copy.6
  (2 shorter events, 0.0 us)
Async XLA Ops:
  7.2 1.6 copy-start
  7.2 82.2 %all-reduce.4.cloned.1.call-start = ((), (), s32[]{:S(2)}) async-start(), calls=%async_computation | async-start | bytes 2097152 | tf_op jit(solution)/shard_map/psum | solution.py:31
  18.7 256.6 %all-reduce.6.cloned.1.call-start = ((), (), s32[]{:S(2)}) async-start(), calls=%async_computation.1 | async-start | bytes 4194304 | tf_op jit(solution)/shard_map/psum | solution.py:35
  100.1 287.4 %all-reduce.8.cloned.1.call-start = ((), (), s32[]{:S(2)}) async-start(), calls=%async_computation.2 | async-start | bytes 524288 | tf_op jit(solution)/shard_map/psum | solution.py:39
  275.3 42.1 %copy-start.2 = (f32[2048,256]{0,1:T(8,128)S(1)}, f32[2048,256]{0,1:T(8,128)}, u32[]{:S(2)}) copy-start(f32[2048,256]{0,1:T(8,128)} %all-reduce.6.cloned.1.call-done) | copy-start | bytes 6291460
  277.2 40.2 %collective-permute-start = (f32[2048,256]{0,1:T(8,128)S(1)}, f32[2048,256]{0,1:T(8,128)S(1)}, u32[]{:S(2)}, u32[]{:S(2)}) collective-permute-start(f32[2048,256]{0,1:T(8,128)S(1)} %broadcast_multiply_fusion), channel_id=1, source_target_pairs={{0,1},{1,0},{2,3},{3,2},{4,5},{5,4},{6,7},{7,6},{8,9},{9,8},{10,11... | collective-permute-start | bytes 6291464 | tf_op jit(solution)/shard_map/ppermute | solution.py:11
  318.3 1.3 copy-start.1
Sparse Core Ops, SparseCore 0:
  18.8 70.5 all-reduce.3
  100.2 175.0 all-reduce.5
  322.3 65.1 all-reduce.7
where the time goes:
time: 396 us
  waiting for transfers between devices  347 us (88%)
  matrix products  23.2 us (6%)
  between operations  13.8 us (3%)
  local copies, waits for them, and re-layouts  5.38 us (1%)
    psum x1, waiting for transfers between devices, local(): covariance = lax.psum(local_cov, 'particle') * factor  175 us
    psum x1, waiting for transfers between devices, local(): scores = lax.psum(partial_value, 'coeffici')  70.6 us
    psum x1, waiting for transfers between devices, local(): rayleigh = lax.psum(correlation, 'coeffici') * factor  63.6 us
    ppermute x1, waiting for transfers between devices, from_partner(): return lax.ppermute(value, axis, pairs)  38 us
    dot_general x2, matrix products, contract_rows(): lax.dot_general(left, right, (((0,), (0,)), ((), ())), precision=lax.Prec...  13.3 us
    dot_general x1, matrix products, local(): jnp.dot(samples, loading, precision=lax.Precision.HIGHEST, preferred_elem...  9.87 us
  transfers between devices with their start and end apart: 4, of which 4 were waited for; matrix products, arithmetic and copies ran while one was open for 0% of the time, Pallas kernels for 0%

commit v1 on v0

--- a/solution.py
+++ b/solution.py
@@ -3,6 +3,14 @@
 import jax.numpy as jnp
 from jax import lax
 from jax.sharding import PartitionSpec as P
+
+
+def added_up(shard, name):
+    peers, result = (lax.axis_size(name), shard)
+    for hop in [1 << k for k in range(peers.bit_length() - 1)]:
+        swap = [(i, i ^ hop) for i in range(peers)]
+        result = result + lax.ppermute(result, name, swap)
+    return result
 
 
 def from_partner(value, axis, distance):
@@ -28,7 +36,7 @@
     partial_value = jnp.dot(
         samples, loading, precision=lax.Precision.HIGHEST, preferred_element_type=jnp.float32
     )
-    scores = lax.psum(partial_value, "coeffici")
+    scores = added_up(partial_value, "coeffici")
     share_rows = samples.shape[1] // lax.axis_size("particle")
     first_row = lax.axis_index("particle") * share_rows
     local_cov = contract_rows(samples, scores)

time: 396 us -> 382 us (0.965)
  waiting for transfers between devices: 347 us -> 329 us
  starting transfers between devices: 2.28 us -> 7.18 us
    psum x1 -> x0, waiting for transfers between devices: 70.6 us -> none  [local(): scores = lax.psum(partial_value, 'coeffici')]
    ppermute x0 -> x3, waiting for transfers between devices: none -> 49.2 us  [added_up(): result = result + lax.ppermute(result, name, swap)]
    ppermute x0 -> x3, starting transfers between devices: none -> 4.95 us  [added_up(): result = result + lax.ppermute(result, name, swap)]
  transfers between devices with their start and end apart: 4 -> 6, of which waited for: 4 -> 6; matrix products, arithmetic and copies ran while one was open for 0% -> 0% of each run, Pallas kernels for 0% -> 0%
where the time goes in v1:
time: 382 us; the launch traced here: 381 us
  waiting for transfers between devices  329 us (86%)
  matrix products  21.1 us (6%)
  between operations  14.1 us (4%)
  starting transfers between devices  7.18 us (2%)
  local copies, waits for them, and re-layouts  5.4 us (1%)
  other arithmetic  4.05 us (1%)
    psum x1, waiting for transfers between devices, local(): covariance = lax.psum(local_cov, 'particle') * factor  179 us
    psum x1, waiting for transfers between devices, local(): rayleigh = lax.psum(correlation, 'coeffici') * factor  63.6 us
    ppermute x3, waiting for transfers between devices, added_up(): result = result + lax.ppermute(result, name, swap)  49.2 us
    ppermute x1, waiting for transfers between devices, from_partner(): return lax.ppermute(value, axis, pairs)  38 us
    dot_general x2, matrix products, contract_rows(): lax.dot_general(left, right, (((0,), (0,)), ((), ())), precision=lax.Prec...  11.2 us
    dot_general x1, matrix products, local(): jnp.dot(samples, loading, precision=lax.Precision.HIGHEST, preferred_elem...  9.96 us
  transfers between devices with their start and end apart: 6, of which 6 were waited for; matrix products, arithmetic and copies ran while one was open for 0% of the time, Pallas kernels for 0%

profile of v1, /device:TPU:8, one launch (start us, length us, event | category | flops | bytes accessed | tf_op | source)
XLA Modules:
  0.0 381.4 jit_solution(5462337412020420330)
XLA Ops:
  7.2 1.5 copy-done
  8.8 10.0 %fusion.2 = f32[1024,256]{1,0:T(8,128)S(1)} fusion(f32[1,1024,2048]{2,1,0:T(8,128)} %param.2, f32[1,2048,256]{2,1,0:T(8,128)S(1)} %copy-done), kind=kOutput, calls=%fused_computation.2 | convolution fusion | flops 6442450944 | bytes 11534336 | tf_op jit(solution)/shard_map/dot_general | solution.py:36
  18.7 0.1 collective-permute-start
  18.8 2.6 collective-permute-done
  21.5 0.1 add.19
  21.6 1.6 collective-permute-start.1
  23.2 23.7 %collective-permute-done.1 = f32[1024,256]{1,0:T(8,128)S(1)} collective-permute-done((f32[1024,256]{1,0:T(8,128)S(1)}, f32[1024,256]{1,0:T(8,128)S(1)}, u32[]{:S(2)}, u32[]{:S(2)}) %collective-permute-start.1) | collective-permute-done | bytes 1048608 | tf_op jit(solution)/shard_map/ppermute | solution.py:12
  46.9 0.1 add.20
  47.0 3.3 collective-permute-start.2
  50.3 22.8 %collective-permute-done.2 = f32[1024,256]{1,0:T(8,128)S(1)} collective-permute-done((f32[1024,256]{1,0:T(8,128)S(1)}, f32[1024,256]{1,0:T(8,128)S(1)}, u32[]{:S(2)}, u32[]{:S(2)}) %collective-permute-start.2) | collective-permute-done | bytes 1048608 | tf_op jit(solution)/shard_map/ppermute | solution.py:12
  73.2 8.6 %fusion.4 = f32[2048,256]{0,1:T(8,128)} fusion(f32[1,1024,2048]{2,1,0:T(8,128)S(1)} %copy-done.1, f32[1024,256]{1,0:T(8,128)S(1)} %add.20, f32[1024,256]{1,0:T(8,128)S(1)} %collective-permute-done.2), kind=kOutput, calls=%fused_computation.4 | convolution fusion | flops 6442713088 | bytes 12582912 | tf_op jit(solution)/shard_map/dot_general | solution.py:23
  81.7 0.0 all-reduce.5.cloned.1.call-start
  81.8 178.7 %all-reduce.3.cloned.1.call-done = f32[2048,256]{0,1:T(8,128)} async-done(((f32[2048,256]{0,1:T(8,128)}), f32[2048,256]{0,1:T(8,128)}) %all-reduce.3.cloned.1.call-update) | async-done | bytes 2097168 | tf_op jit(solution)/shard_map/psum | solution.py:43
  260.5 1.9 broadcast_multiply_fusion
  262.4 2.2 collective-permute-start.3
  264.5 38.0 %collective-permute-done.3 = f32[2048,256]{0,1:T(8,128)S(1)} collective-permute-done((f32[2048,256]{0,1:T(8,128)S(1)}, f32[2048,256]{0,1:T(8,128)S(1)}, u32[]{:S(2)}, u32[]{:S(2)}) %collective-permute-start.3) | collective-permute-done | bytes 2097184 | tf_op jit(solution)/shard_map/ppermute | solution.py:19
  302.5 0.9 divide_multiply_fusion
  303.5 1.3 copy-done.2
  304.8 2.6 fusion.10
  307.4 0.9 constant_dynamic-slice_fusion
  308.4 0.8 copy.5
  309.1 63.6 %all-reduce.5.cloned.1.call-done = f32[256,256]{0,1:T(8,128)} async-done(((f32[256,256]{0,1:T(8,128)}), f32[256,256]{0,1:T(8,128)}) %all-reduce.5.cloned.1.call-update) | async-done | bytes 262160 | tf_op jit(solution)/shard_map/psum | solution.py:47
  372.7 1.0 multiply_bitcast_fusion
  373.7 0.8 copy.6
  (9 shorter events, 0.1 us)
Async XLA Ops:
  7.2 1.6 copy-start
  7.2 253.3 %all-reduce.3.cloned.1.call-start = ((), (), s32[]{:S(2)}) async-start(), calls=%async_computation | async-start | bytes 4194304 | tf_op jit(solution)/shard_map/psum | solution.py:43
  8.8 64.4 %copy-start.1 = (f32[1,1024,2048]{2,1,0:T(8,128)S(1)}, f32[1,1024,2048]{2,1,0:T(8,128)}, u32[]{:S(2)}) copy-start(f32[1,1024,2048]{2,1,0:T(8,128)} %param.2) | copy-start | bytes 25165828
  18.7 2.7 collective-permute-start
  21.6 25.3 %collective-permute-start.1 = (f32[1024,256]{1,0:T(8,128)S(1)}, f32[1024,256]{1,0:T(8,128)S(1)}, u32[]{:S(2)}, u32[]{:S(2)}) collective-permute-start(f32[1024,256]{1,0:T(8,128)S(1)} %add.19), channel_id=1, source_target_pairs={{0,4},{2,6},{4,0},{6,2},{8,12},{10,14},{12,8},{14,10},{1,5},{3,7},... | collective-permute-start | bytes 3145736 | tf_op jit(solution)/shard_map/ppermute | solution.py:12
  47.0 26.1 %collective-permute-start.2 = (f32[1024,256]{1,0:T(8,128)S(1)}, f32[1024,256]{1,0:T(8,128)S(1)}, u32[]{:S(2)}, u32[]{:S(2)}) collective-permute-start(f32[1024,256]{1,0:T(8,128)S(1)} %add.20), channel_id=1, source_target_pairs={{0,8},{2,10},{4,12},{6,14},{8,0},{10,2},{12,4},{14,6},{1,9},{3,11}... | collective-permute-start | bytes 3145736 | tf_op jit(solution)/shard_map/ppermute | solution.py:12
  81.7 291.0 %all-reduce.5.cloned.1.call-start = ((), (), s32[]{:S(2)}) async-start(), calls=%async_computation.1 | async-start | bytes 524288 | tf_op jit(solution)/shard_map/psum | solution.py:47
  260.5 42.1 %copy-start.3 = (f32[2048,256]{0,1:T(8,128)S(1)}, f32[2048,256]{0,1:T(8,128)}, u32[]{:S(2)}) copy-start(f32[2048,256]{0,1:T(8,128)} %all-reduce.3.cloned.1.call-done) | copy-start | bytes 6291460
  262.4 40.2 %collective-permute-start.3 = (f32[2048,256]{0,1:T(8,128)S(1)}, f32[2048,256]{0,1:T(8,128)S(1)}, u32[]{:S(2)}, u32[]{:S(2)}) collective-permute-start(f32[2048,256]{0,1:T(8,128)S(1)} %broadcast_multiply_fusion), channel_id=1, source_target_pairs={{0,1},{1,0},{2,3},{3,2},{4,5},{5,4},{6,7},{7,6},{8,9},{9,8},{10,11... | collective-permute-start | bytes 6291464 | tf_op jit(solution)/shard_map/ppermute | solution.py:19
  303.4 1.3 copy-start.2
Sparse Core Ops, SparseCore 0:
  81.9 178.5 all-reduce.2
  307.6 65.1 all-reduce.4
